TPU v7x, 128 devices: a whole 4x4x4 slice. The times are simulated.
128 devices in a mesh: row: 8 (over y, z_lo), col: 16 (over x, z_hi, core).
Axes of the slice: x: 4, y: 4, z: 4 (z_hi: 2, z_lo: 2; z = z_hi * 2 + z_lo), core: 2. Of those that a mesh axis runs over, the one named last changes fastest.
Arguments:
- spectra: bfloat16 [4096, 8, 1536], P(('row', 'col')), may hold values from -6 to 6
- pair_bins: int32 [4, 4096, 32], P(None, ('row', 'col')), may hold values from 0 to 127
- dead_mask: int32 [4096], P(('row', 'col')), may hold values 0 or 1
Outputs:
- stacked_lags: float32 [128, 896], P(('row', 'col'))
All inputs are finite; a program needn't handle non-finite values. No bound on the sum of `dead_mask` on one device may be relied on, other than what follows from the above.
Results may differ from a plain program's by a relative error of at most 0.0041.
Values may be sent and summed in bfloat16 or wider, within the bound.
A program may use at most 256 MiB of HBM per device.

v0:
```python
import math

import jax
import jax.numpy as jnp
from jax import lax
from jax.sharding import PartitionSpec as P

NT = 1600
LAGS = 896
NB = 128
ROUNDS = 4


def swapped(value, axis, stride):
    mask = 2**stride
    pairs = [(source, source ^ mask) for source in range(lax.axis_size(axis))]
    return lax.ppermute(value, axis, pairs)


def whiten(spectra, dead_mask):
    values = spectra.astype(jnp.float32)
    powers = jnp.mean(values * values, axis=-1, keepdims=True)
    alive = dead_mask.astype(jnp.float32)[:, None, None]
    return (values / jnp.sqrt(powers + 1e-06) * alive).astype(jnp.bfloat16)


def cross_spectra(local_part, remote_part):
    half_len = local_part.shape[-1] // 2
    one_real, one_imag = (local_part[..., :half_len], local_part[..., half_len:])
    two_real, two_imag = (remote_part[..., :half_len], remote_part[..., half_len:])
    real_part = jnp.einsum(
        "iwk,jwk->ijk", one_real, two_real, preferred_element_type=jnp.float32
    ) + jnp.einsum("iwk,jwk->ijk", one_imag, two_imag, preferred_element_type=jnp.float32)
    imag_part = jnp.einsum(
        "iwk,jwk->ijk", one_imag, two_real, preferred_element_type=jnp.float32
    ) - jnp.einsum("iwk,jwk->ijk", one_real, two_imag, preferred_element_type=jnp.float32)
    channels = local_part.shape[0]
    return jnp.concatenate([real_part, imag_part], axis=-1).reshape(
        channels * remote_part.shape[0], 2 * half_len
    )


def build_table(freq_len, lag_len, length):
    freq_ids = jnp.arange(freq_len, dtype=jnp.int32)
    lag_ids = jnp.arange(lag_len, dtype=jnp.int32) - lag_len // 2
    phases = freq_ids[:, None] * lag_ids[None, :] % length
    angles = phases.astype(jnp.float32) * (2.0 * math.pi / length)
    weights = jnp.where(freq_ids == 0, 1.0, 2.0).astype(jnp.float32)[:, None]
    return jnp.concatenate([weights * jnp.cos(angles), -weights * jnp.sin(angles)], axis=0)


def one_hot_bins(bin_ids):
    bin_range = jnp.arange(NB, dtype=jnp.int32)
    return (bin_ids.reshape(-1)[:, None] == bin_range[None, :]).astype(jnp.float32)


def stack_bins(hot_rows, values):
    return lax.dot_general(
        hot_rows, values, (((0,), (0,)), ((), ())), precision=lax.Precision.HIGHEST
    )


def on_device(spectra, pair_bins, dead_mask):
    whitened = whiten(spectra, dead_mask)
    block_size = spectra.shape[0]
    width = spectra.shape[1]
    freq_len = spectra.shape[2] // 2
    groups = lax.axis_size("row") * lax.axis_size("col")
    stacked = jnp.zeros((NB, 2 * freq_len), jnp.float32)
    for round_no in range(ROUNDS):
        remote_part = swapped(whitened, ("row", "col"), round_no)
        stacked = stacked + stack_bins(
            one_hot_bins(pair_bins[round_no]), cross_spectra(whitened, remote_part)
        )
    pairs = ROUNDS * block_size * block_size * groups // NB
    scaling = 1.0 / (2.0 * math.sqrt(freq_len * width * pairs))
    table = build_table(freq_len, LAGS, NT)
    owned = lax.psum_scatter(stacked, ("row", "col"), scatter_dimension=0, tiled=True)
    result = jnp.dot(owned, table, precision=lax.Precision.HIGHEST) * scaling
    return result


def solution(mesh):
    return jax.shard_map(
        on_device,
        mesh=mesh,
        in_specs=(P(("row", "col"), None, None), P(None, ("row", "col"), None), P(("row", "col"))),
        out_specs=P(("row", "col"), None),
        check_vma=False,
    )
```

profile of v0, /device:TPU:1, one launch (start us, length us, event | category | flops | bytes accessed | tf_op | source)
XLA Modules:
  0.0 452.8 jit_solution(2164464155440805291)
XLA Ops:
  6.5 1.4 fusion.9
  7.9 0.7 convert_element_type.19
  8.6 2.3 fusion.11
  10.9 1.4 collective-permute-start
  12.3 3.7 collective-permute-start.1
  16.0 1.2 collective-permute-start.2
  17.2 2.5 collective-permute-start.3
  19.6 1.2 fusion.29
  20.8 1.2 copy.34
  22.0 1.2 copy.32
  23.1 0.8 fusion.31
  24.0 0.7 eq.81
  24.7 0.7 eq.85
  25.3 0.7 eq.89
  26.6 1.9 fusion.30
  28.5 3.0 copy.64
  31.5 6.8 %fusion.32 = f32[768,32,32]{2,1,0:T(8,128)} fusion(bf16[32,8,768]{0,1,2:T(8,128)(2,1)} %copy.64, bf16[32,8,768]{0,1,2:T(8,128)(2,1)S(1)} %copy.34), kind=kOutput, calls=%fused_computation.59 | convolution fusion | flops 12582912 | bytes 3932160 | tf_op jit(solution)/shard_map/iwk,jwk->ijk/dot_general | solution.py:33
  38.4 5.5 %fusion.33 = f32[768,32,32]{2,1,0:T(8,128)} fusion(bf16[32,8,768]{0,1,2:T(8,128)(2,1)S(1)} %copy-done.1, bf16[32,8,768]{0,1,2:T(8,128)(2,1)S(1)} %copy.32), kind=kOutput, calls=%fused_computation.60 | convolution fusion | flops 12582912 | bytes 3932160 | tf_op jit(solution)/shard_map/iwk,jwk->ijk/dot_general | solution.py:36
  43.9 2.0 fusion.28
  45.9 3.0 copy.66
  48.9 6.8 %fusion.34 = f32[768,32,32]{2,1,0:T(8,128)} fusion(bf16[32,8,768]{0,1,2:T(8,128)(2,1)} %copy.66, bf16[32,8,768]{0,1,2:T(8,128)(2,1)S(1)} %copy.34), kind=kOutput, calls=%fused_computation.61 | convolution fusion | flops 12582912 | bytes 3932160 | tf_op jit(solution)/shard_map/iwk,jwk->ijk/dot_general | solution.py:33
  55.7 5.5 %fusion.35 = f32[768,32,32]{2,1,0:T(8,128)} fusion(bf16[32,8,768]{0,1,2:T(8,128)(2,1)S(1)} %copy-done.2, bf16[32,8,768]{0,1,2:T(8,128)(2,1)S(1)} %copy.32), kind=kOutput, calls=%fused_computation.62 | convolution fusion | flops 12582912 | bytes 3932160 | tf_op jit(solution)/shard_map/iwk,jwk->ijk/dot_general | solution.py:36
  61.2 2.0 fusion.27
  63.3 3.0 copy.68
  66.3 6.8 %fusion.36 = f32[768,32,32]{2,1,0:T(8,128)} fusion(bf16[32,8,768]{0,1,2:T(8,128)(2,1)} %copy.68, bf16[32,8,768]{0,1,2:T(8,128)(2,1)S(1)} %copy.34), kind=kOutput, calls=%fused_computation.63 | convolution fusion | flops 12582912 | bytes 3932160 | tf_op jit(solution)/shard_map/iwk,jwk->ijk/dot_general | solution.py:33
  73.0 5.5 %fusion.37 = f32[768,32,32]{2,1,0:T(8,128)} fusion(bf16[32,8,768]{0,1,2:T(8,128)(2,1)S(1)} %copy-done.3, bf16[32,8,768]{0,1,2:T(8,128)(2,1)S(1)} %copy.32), kind=kOutput, calls=%fused_computation.64 | convolution fusion | flops 12582912 | bytes 3932160 | tf_op jit(solution)/shard_map/iwk,jwk->ijk/dot_general | solution.py:36
  78.5 2.1 fusion.26
  80.5 3.0 copy.70
  83.6 6.9 %fusion.38 = f32[768,32,32]{2,1,0:T(8,128)} fusion(bf16[32,8,768]{0,1,2:T(8,128)(2,1)} %copy.70, bf16[32,8,768]{0,1,2:T(8,128)(2,1)S(1)} %copy.34), kind=kOutput, calls=%fused_computation.65 | convolution fusion | flops 12582912 | bytes 3932160 | tf_op jit(solution)/shard_map/iwk,jwk->ijk/dot_general | solution.py:33
  90.4 5.4 %fusion.39 = f32[768,32,32]{2,1,0:T(8,128)} fusion(bf16[32,8,768]{0,1,2:T(8,128)(2,1)S(1)} %copy-done.4, bf16[32,8,768]{0,1,2:T(8,128)(2,1)S(1)} %copy.32), kind=kOutput, calls=%fused_computation.66 | convolution fusion | flops 12582912 | bytes 3932160 | tf_op jit(solution)/shard_map/iwk,jwk->ijk/dot_general | solution.py:36
  95.9 1.9 copy.63
  97.8 8.8 %add_bitcast_fusion.3 = f32[32,32,768]{0,1,2:T(8,128)} fusion(f32[768,32,32]{2,1,0:T(8,128)} %fusion.32, bf16[32,8,768]{0,1,2:T(8,128)(2,1)} %copy.63, bf16[32,8,768]{0,1,2:T(8,128)(2,1)S(1)} %copy.32), kind=kOutput, calls=%fused_computation.7 | convolution fusion | flops 13369344 | bytes 7077888 | tf_op jit(solution)/shard_map/iwk,jwk->ijk/dot_general | solution.py:31
  106.6 11.3 %copy.37 = f32[32,32,768]{2,1,0:T(8,128)} copy(f32[32,32,768]{0,1,2:T(8,128)} %add_bitcast_fusion.3) | data formatting | bytes 6291456 | tf_op jit(solution)/shard_map/add | solution.py:31
  117.9 8.7 %subtract_bitcast_fusion.3 = f32[32,32,768]{0,1,2:T(8,128)} fusion(f32[768,32,32]{2,1,0:T(8,128)} %fusion.33, bf16[32,8,768]{0,1,2:T(8,128)(2,1)} %copy.63, bf16[32,8,768]{0,1,2:T(8,128)(2,1)S(1)} %copy.34), kind=kOutput, calls=%fused_computation.6 | convolution fusion | flops 13369344 | bytes 7077888 | tf_op jit(solution)/shard_map/iwk,jwk->ijk/dot_general | solution.py:34
  126.6 11.1 %copy.38 = f32[32,32,768]{2,1,0:T(8,128)} copy(f32[32,32,768]{0,1,2:T(8,128)} %subtract_bitcast_fusion.3) | data formatting | bytes 6291456 | tf_op jit(solution)/shard_map/sub | solution.py:34
  137.7 1.9 copy.65
  139.6 8.7 %add_bitcast_fusion.2 = f32[32,32,768]{0,1,2:T(8,128)} fusion(f32[768,32,32]{2,1,0:T(8,128)} %fusion.34, bf16[32,8,768]{0,1,2:T(8,128)(2,1)} %copy.65, bf16[32,8,768]{0,1,2:T(8,128)(2,1)S(1)} %copy.32), kind=kOutput, calls=%fused_computation.5 | convolution fusion | flops 13369344 | bytes 7077888 | tf_op jit(solution)/shard_map/iwk,jwk->ijk/dot_general | solution.py:31
  148.3 11.0 %copy.45 = f32[32,32,768]{2,1,0:T(8,128)} copy(f32[32,32,768]{0,1,2:T(8,128)} %add_bitcast_fusion.2) | data formatting | bytes 6291456 | tf_op jit(solution)/shard_map/add | solution.py:31
  159.3 8.7 %subtract_bitcast_fusion.2 = f32[32,32,768]{0,1,2:T(8,128)} fusion(f32[768,32,32]{2,1,0:T(8,128)} %fusion.35, bf16[32,8,768]{0,1,2:T(8,128)(2,1)} %copy.65, bf16[32,8,768]{0,1,2:T(8,128)(2,1)S(1)} %copy.34), kind=kOutput, calls=%fused_computation.4 | convolution fusion | flops 13369344 | bytes 7077888 | tf_op jit(solution)/shard_map/iwk,jwk->ijk/dot_general | solution.py:34
  168.0 11.1 %copy.46 = f32[32,32,768]{2,1,0:T(8,128)} copy(f32[32,32,768]{0,1,2:T(8,128)} %subtract_bitcast_fusion.2) | data formatting | bytes 6291456 | tf_op jit(solution)/shard_map/sub | solution.py:34
  179.1 1.9 copy.67
  181.0 8.7 %add_bitcast_fusion.1 = f32[32,32,768]{0,1,2:T(8,128)} fusion(f32[768,32,32]{2,1,0:T(8,128)} %fusion.36, bf16[32,8,768]{0,1,2:T(8,128)(2,1)} %copy.67, bf16[32,8,768]{0,1,2:T(8,128)(2,1)S(1)} %copy.32), kind=kOutput, calls=%fused_computation.3 | convolution fusion | flops 13369344 | bytes 7077888 | tf_op jit(solution)/shard_map/iwk,jwk->ijk/dot_general | solution.py:31
  189.7 11.0 %copy.53 = f32[32,32,768]{2,1,0:T(8,128)} copy(f32[32,32,768]{0,1,2:T(8,128)} %add_bitcast_fusion.1) | data formatting | bytes 6291456 | tf_op jit(solution)/shard_map/add | solution.py:31
  200.7 8.7 %subtract_bitcast_fusion.1 = f32[32,32,768]{0,1,2:T(8,128)} fusion(f32[768,32,32]{2,1,0:T(8,128)} %fusion.37, bf16[32,8,768]{0,1,2:T(8,128)(2,1)} %copy.67, bf16[32,8,768]{0,1,2:T(8,128)(2,1)S(1)} %copy.34), kind=kOutput, calls=%fused_computation.2 | convolution fusion | flops 13369344 | bytes 7077888 | tf_op jit(solution)/shard_map/iwk,jwk->ijk/dot_general | solution.py:34
  209.5 23.0 %copy.54 = f32[32,32,768]{2,1,0:T(8,128)} copy(f32[32,32,768]{0,1,2:T(8,128)} %subtract_bitcast_fusion.1) | data formatting | bytes 6291456 | tf_op jit(solution)/shard_map/sub | solution.py:34
  232.5 1.9 copy.69
  234.4 8.8 %add_bitcast_fusion = f32[32,32,768]{0,1,2:T(8,128)} fusion(f32[768,32,32]{2,1,0:T(8,128)} %fusion.38, bf16[32,8,768]{0,1,2:T(8,128)(2,1)} %copy.69, bf16[32,8,768]{0,1,2:T(8,128)(2,1)S(1)} %copy.32), kind=kOutput, calls=%fused_computation.1 | convolution fusion | flops 13369344 | bytes 7077888 | tf_op jit(solution)/shard_map/iwk,jwk->ijk/dot_general | solution.py:31
  243.2 11.2 %copy.61 = f32[32,32,768]{2,1,0:T(8,128)} copy(f32[32,32,768]{0,1,2:T(8,128)} %add_bitcast_fusion) | data formatting | bytes 6291456 | tf_op jit(solution)/shard_map/add | solution.py:31
  254.4 8.3 %subtract_bitcast_fusion = f32[32,32,768]{0,1,2:T(8,128)} fusion(f32[768,32,32]{2,1,0:T(8,128)} %fusion.39, bf16[32,8,768]{0,1,2:T(8,128)(2,1)S(1)} %copy-done, bf16[32,8,768]{0,1,2:T(8,128)(2,1)S(1)} %copy.34), kind=kOutput, calls=%fused_computation | convolution fusion | flops 13369344 | bytes 7077888 | tf_op jit(solution)/shard_map/iwk,jwk->ijk/dot_general | solution.py:34
  262.7 11.1 %copy.62 = f32[32,32,768]{2,1,0:T(8,128)} copy(f32[32,32,768]{0,1,2:T(8,128)} %subtract_bitcast_fusion) | data formatting | bytes 6291456 | tf_op jit(solution)/shard_map/sub | solution.py:34
  273.8 3.6 pad_maximum_fusion
  277.4 2.5 fusion.15
  280.2 0.8 pad_maximum_fusion.1
  281.1 1.1 copy-done.7
  282.1 1.0 copy-done.8
  283.1 0.8 pad_maximum_fusion.2
  283.9 1.1 copy-done.9
  285.0 2.6 pad_maximum_fusion.3
  287.6 2.5 convolution_add_fusion.2
  290.1 2.5 convolution_add_fusion.1
  292.6 3.4 convolution_add_fusion
  296.1 12.6 %cosine_multiply_fusion = (f32[768,896]{1,0:T(8,128)}, f32[768,896]{1,0:T(8,128)}) fusion(s32[896]{0:T(1024)S(1)} %iota_add_fusion, f32[768]{0:T(1024)S(1)} %copy-done.16, f32[768]{0:T(1024)S(1)} %copy-done.17), kind=kLoop, calls=%fused_computation.20 | loop fusion | flops 7569408 | bytes 5514752 | tf_op jit(solution)/shard_map/mul | solution.py:49
  308.7 131.2 %all-reduce.3.cloned.1.call-done = f32[128,1536]{1,0:T(8,128)} async-done(((f32[128,1536]{1,0:T(8,128)}), f32[128,1536]{1,0:T(8,128)}) %all-reduce.3.cloned.1.call-update) | async-done | bytes 786448
  439.9 5.3 %fusion.12 = f32[896]{0:T(1024)S(1)} fusion(f32[768,896]{1,0:T(8,128)} %get-tuple-element.20, f32[768,896]{1,0:T(8,128)} %get-tuple-element.19, f32[128,1536]{1,0:T(8,128)} %all-reduce.3.cloned.1.call-done, u32[]{:T(128)S(6)} %add.74), kind=kOutput, calls=%fused_computation.33 | convolution fusion | flops 17891328 | bytes 5514756 | tf_op jit(solution)/shard_map/dot_general | solution.py:79
  (45 shorter events, 1.7 us)
Async XLA Ops:
  6.5 433.4 %all-reduce.3.cloned.1.call-start = ((), (), s32[]{:S(2)}) async-start(), calls=%async_computation | async-start | bytes 1572864
  10.9 15.7 %collective-permute-start = (bf16[32,8,1536]{2,1,0:T(8,128)(2,1)}, bf16[32,8,1536]{2,1,0:T(8,128)(2,1)}, u32[]{:S(2)}, u32[]{:S(2)}) collective-permute-start(bf16[32,8,1536]{2,1,0:T(8,128)(2,1)} %fusion.11), channel_id=1, source_target_pairs={{0,1},{1,0},{2,3},{3,2},{4,5},{5,4},{6,7},{7,6},{8,9},{9,8},{10,11... | collective-permute-start | bytes 2359304 | tf_op jit(solution)/shard_map/ppermute | solution.py:17
  12.3 31.6 %collective-permute-start.1 = (bf16[32,8,1536]{2,1,0:T(8,128)(2,1)}, bf16[32,8,1536]{2,1,0:T(8,128)(2,1)}, u32[]{:S(2)}, u32[]{:S(2)}) collective-permute-start(bf16[32,8,1536]{2,1,0:T(8,128)(2,1)} %fusion.11), channel_id=1, source_target_pairs={{0,2},{1,3},{2,0},{3,1},{4,6},{5,7},{6,4},{7,5},{8,10},{9,11},{10,... | collective-permute-start | bytes 2359304 | tf_op jit(solution)/shard_map/ppermute | solution.py:17
  16.0 45.2 %collective-permute-start.2 = (bf16[32,8,1536]{2,1,0:T(8,128)(2,1)}, bf16[32,8,1536]{2,1,0:T(8,128)(2,1)}, u32[]{:S(2)}, u32[]{:S(2)}) collective-permute-start(bf16[32,8,1536]{2,1,0:T(8,128)(2,1)} %fusion.11), channel_id=1, source_target_pairs={{0,4},{1,5},{2,6},{3,7},{4,0},{5,1},{6,2},{7,3},{8,12},{9,13},{10,... | collective-permute-start | bytes 2359304 | tf_op jit(solution)/shard_map/ppermute | solution.py:17
  17.2 61.3 %collective-permute-start.3 = (bf16[32,8,1536]{2,1,0:T(8,128)(2,1)}, bf16[32,8,1536]{2,1,0:T(8,128)(2,1)}, u32[]{:S(2)}, u32[]{:S(2)}) collective-permute-start(bf16[32,8,1536]{2,1,0:T(8,128)(2,1)} %fusion.11), channel_id=1, source_target_pairs={{0,8},{1,9},{2,10},{3,11},{4,12},{5,13},{6,14},{7,15},{8,0},{9,1},... | collective-permute-start | bytes 2359304 | tf_op jit(solution)/shard_map/ppermute | solution.py:17
  31.5 6.8 %copy-start.1 = (bf16[32,8,768]{0,1,2:T(8,128)(2,1)S(1)}, bf16[32,8,768]{0,1,2:T(8,128)(2,1)}, u32[]{:S(2)}) copy-start(bf16[32,8,768]{0,1,2:T(8,128)(2,1)} %copy.64) | copy-start | bytes 1179652
  48.9 6.8 %copy-start.2 = (bf16[32,8,768]{0,1,2:T(8,128)(2,1)S(1)}, bf16[32,8,768]{0,1,2:T(8,128)(2,1)}, u32[]{:S(2)}) copy-start(bf16[32,8,768]{0,1,2:T(8,128)(2,1)} %copy.66) | copy-start | bytes 1179652
  66.3 6.8 %copy-start.3 = (bf16[32,8,768]{0,1,2:T(8,128)(2,1)S(1)}, bf16[32,8,768]{0,1,2:T(8,128)(2,1)}, u32[]{:S(2)}) copy-start(bf16[32,8,768]{0,1,2:T(8,128)(2,1)} %copy.68) | copy-start | bytes 1179652
  83.6 6.9 %copy-start.4 = (bf16[32,8,768]{0,1,2:T(8,128)(2,1)S(1)}, bf16[32,8,768]{0,1,2:T(8,128)(2,1)}, u32[]{:S(2)}) copy-start(bf16[32,8,768]{0,1,2:T(8,128)(2,1)} %copy.70) | copy-start | bytes 1179652
  126.6 11.1 %copy-start.10 = (bf16[32,8,768]{2,1,0:T(8,128)(2,1)S(1)}, bf16[32,8,768]{2,1,0:T(8,128)(2,1)}, u32[]{:S(2)}) copy-start(bf16[32,8,768]{2,1,0:T(8,128)(2,1)} %get-tuple-element.9) | copy-start | bytes 1179652
  168.0 11.1 %copy-start.11 = (bf16[32,8,768]{2,1,0:T(8,128)(2,1)S(1)}, bf16[32,8,768]{2,1,0:T(8,128)(2,1)}, u32[]{:S(2)}) copy-start(bf16[32,8,768]{2,1,0:T(8,128)(2,1)} %get-tuple-element.7) | copy-start | bytes 1179652
  209.5 23.0 %copy-start.12 = (bf16[32,8,768]{2,1,0:T(8,128)(2,1)S(1)}, bf16[32,8,768]{2,1,0:T(8,128)(2,1)}, u32[]{:S(2)}) copy-start(bf16[32,8,768]{2,1,0:T(8,128)(2,1)} %get-tuple-element.5) | copy-start | bytes 1179652
  243.2 11.2 %copy-start = (bf16[32,8,768]{0,1,2:T(8,128)(2,1)S(1)}, bf16[32,8,768]{0,1,2:T(8,128)(2,1)}, u32[]{:S(2)}) copy-start(bf16[32,8,768]{0,1,2:T(8,128)(2,1)} %copy.69) | copy-start | bytes 1179652
  277.4 2.5 copy-start.5
  277.4 2.8 copy-start.6
  280.2 1.9 copy-start.7
  280.2 2.8 copy-start.8
  283.1 1.9 copy-start.9
  285.0 2.6 copy-start.15
  287.6 2.5 copy-start.14
  290.1 2.5 copy-start.13
  292.6 3.4 copy-start.16
  292.6 3.4 copy-start.17
Sparse Core Ops, SparseCore 0:
  296.1 143.7 all-reduce.2
where the time goes:
time: 458 us; the launch traced here: 453 us
  local copies, waits for them, and re-layouts  139 us (30%)
  matrix products  135 us (29%)
  waiting for transfers between devices  131 us (29%)
  other arithmetic  25.4 us (6%)
  between operations  13.9 us (3%)
  starting transfers between devices  8.76 us (2%)
    unnamed x2, waiting for transfers between devices  131 us
    sub x4, local copies, waits for them, and re-layouts, cross_spectra(): jnp.einsum('iwk,jwk->ijk', one_imag, two_real, preferred_element_type=jnp...  56.3 us
    add x4, local copies, waits for them, and re-layouts, cross_spectra(): jnp.einsum('iwk,jwk->ijk', one_real, two_real, preferred_element_type=jnp...  44.5 us
    dot_general x4, matrix products, cross_spectra(): jnp.einsum('iwk,jwk->ijk', one_real, two_real, preferred_element_type=jnp...  35 us
    dot_general x4, matrix products, cross_spectra(): jnp.einsum('iwk,jwk->ijk', one_imag, two_real, preferred_element_type=jnp...  34.4 us
    dot_general x4, matrix products, cross_spectra(): jnp.einsum('iwk,jwk->ijk', one_imag, two_imag, preferred_element_type=jnp...  27.3 us
    unnamed x44, local copies, waits for them, and re-layouts  23.2 us
    dot_general x4, matrix products, cross_spectra(): jnp.einsum('iwk,jwk->ijk', one_real, two_imag, preferred_element_type=jnp...  21.9 us
  transfers between devices with their start and end apart: 5, of which 1 were waited for; matrix products, arithmetic and copies ran while one was open for 16% of the time, Pallas kernels for 0%

commit v1 on v0

v1 whole, which is shorter than its diff:
```python
import functools
import math

import jax
import jax.numpy as jnp
import numpy as np
from jax import lax
from jax.experimental import pallas as pl
from jax.experimental.pallas import tpu as pltpu
from jax.sharding import PartitionSpec as P

NT = 1600
LAGS = 896
NB = 128
ROUNDS = 4
CB = 32
W = 8
F = 768
N_ROW = 8
N_COL = 16
FC = 16
HALF = F // 2
CHUNKS = HALF // FC
PIECES = 6
CP = CHUNKS // PIECES
MESH = pl.DeviceIdType.MESH
F32 = jnp.float32
BF16 = jnp.bfloat16


def tables():
    at = np.arange(F, dtype=np.int64)
    k = at // 128 * 128 + -(at % 128 // FC) % 8 * FC + at % FC
    scale = 1.0 / (2.0 * math.sqrt(F * W * (ROUNDS * CB * CB * N_ROW * N_COL // NB)))
    weight = np.where(k == 0, 1.0, 2.0) * scale
    start = 128 * np.arange(8, dtype=np.int64) - LAGS // 2
    first = (start[:, None] * k[None, :] % NT) * (2.0 * np.pi / NT)
    cos1 = (np.cos(first) * weight).reshape(8, 2, HALF).transpose(1, 0, 2)
    sin1 = (np.sin(first) * weight).reshape(8, 2, HALF).transpose(1, 0, 2)
    e1 = np.stack([cos1, sin1], axis=1).astype(np.float32)
    second = (k[:, None] * np.arange(128, dtype=np.int64)[None, :] % NT) * (2.0 * np.pi / NT)
    cos2 = np.cos(second).reshape(2, HALF, 128)
    sin2 = -np.sin(second).reshape(2, HALF, 128)
    e2 = np.concatenate([cos2, sin2], axis=1).astype(np.float32)
    high = e2.astype(jnp.bfloat16)
    low = (e2 - high.astype(np.float32)).astype(jnp.bfloat16)
    return e1, np.stack([high, low], axis=0)


def flip(value, mask):
    for bit in range(4):
        if mask >> bit & 1:
            value = value + (1 << bit) * (1 - 2 * ((value // (1 << bit)) % 2))
    return value


def nt_dot(a, b):
    return lax.dot_general(a, b, (((1,), (1,)), ((), ())), preferred_element_type=F32)


def kernel(
    alive_ref, spec_hbm, bins_ref, e1_hbm, e2_hbm, out_ref,
    x_v, d_v, send_v, recv_v, relay_v, pbs_v, pbr_v, oh_v, cross_v, part_v, rows_v, s2_v, r2_v, e1_v, e2_v,
    local_sem, pb_ss, pb_rs, a_ss, a_rs, f_ss, f_rs, row_ss, row_rs, col_ss, col_rs,
):
    row = lax.axis_index("row")
    col = lax.axis_index("col")
    parity = (col + col // 2 + col // 4 + col // 8) % 2

    def device(mask):
        return (flip(row, mask >> 4), flip(col, mask & 15))

    load = pltpu.make_async_copy(spec_hbm, x_v, local_sem.at[0])
    load.start()
    load_e1 = pltpu.make_async_copy(e1_hbm, e1_v, local_sem.at[1])
    load_e1.start()
    load_e2 = pltpu.make_async_copy(e2_hbm, e2_v, local_sem.at[2])
    load_e2.start()

    peers = sorted({16 * k for k in range(1, 8)} | set(range(1, 16)) | {18})
    barrier = pltpu.get_barrier_semaphore()
    for mask in peers:
        pl.semaphore_signal(barrier, inc=1, device_id=device(mask), device_id_type=MESH)

    bins = bins_ref[...].reshape(ROUNDS * CB, CB)
    padded = jnp.concatenate([bins, jnp.zeros((128, 96), jnp.int32)], axis=1).astype(F32)
    pbs_v[...] = padded.T[:CB, :].astype(jnp.int32)
    load.wait()

    lane = lax.broadcasted_iota(jnp.int32, (8, 128), 1) // 16
    bits = [(lane // (1 << s)) % 2 == 1 for s in range(3)]

    def whiten(i, _):
        x = x_v[i].astype(F32)
        power = jnp.mean(x * x, axis=-1, keepdims=True)
        alive = alive_ref[i].astype(F32)
        y = x * (alive / jnp.sqrt(power + 1e-06))
        for c in range(2):
            for ft in range(6):
                t = y[:, c * F + ft * 128 : c * F + ft * 128 + 128]
                t = pltpu.roll(t, 0, 1, stride=16, stride_axis=0)
                for s in range(3):
                    t = jnp.where(bits[s], pltpu.roll(t, 8 - (1 << s), 0), t)
                d_v[c, pl.ds(ft * 8 * CB + i, 8, stride=CB), :] = t
        return 0

    lax.fori_loop(0, CB, whiten, 0)

    def pack(q, _):
        start = pl.multiple_of(((1 - parity) * CHUNKS + q) * CB, CB)
        for c in range(2):
            send_v[q, :, c * 128 : c * 128 + 128] = d_v[c, pl.ds(start, CB), :].astype(BF16)
        return 0

    lax.fori_loop(0, CHUNKS, pack, 0)

    pl.semaphore_wait(barrier, len(peers))

    bin_copies = [
        pltpu.make_async_remote_copy(
            src_ref=pbs_v, dst_ref=pbr_v.at[r], send_sem=pb_ss.at[r], recv_sem=pb_rs.at[r],
            device_id=device(1 << r), device_id_type=MESH)
        for r in range(ROUNDS)
    ]
    for copy in bin_copies:
        copy.start()

    def span(piece):
        return pl.ds(piece * CP, CP)

    def core_copy(piece):
        return pltpu.make_async_remote_copy(
            src_ref=send_v.at[span(piece)], dst_ref=recv_v.at[0, span(piece)],
            send_sem=a_ss.at[0, piece], recv_sem=a_rs.at[0, piece], device_id=device(1), device_id_type=MESH)

    def x_copy(piece):
        return pltpu.make_async_remote_copy(
            src_ref=send_v.at[span(piece)], dst_ref=recv_v.at[2, span(piece)],
            send_sem=a_ss.at[1, piece], recv_sem=a_rs.at[1, piece], device_id=device(4), device_id_type=MESH)

    def z_device(odd):
        return (flip(row, 1), col + odd * (flip(col, 2) - col))

    def z_copy(piece):
        return pltpu.make_async_remote_copy(
            src_ref=send_v.at[span(piece)], dst_ref=relay_v.at[span(piece)],
            send_sem=a_ss.at[2, piece], recv_sem=a_rs.at[2, piece],
            device_id=z_device(piece % 2), device_id_type=MESH)

    def x_forward(piece):
        return pltpu.make_async_remote_copy(
            src_ref=recv_v.at[2, span(piece)], dst_ref=recv_v.at[3, span(piece)],
            send_sem=f_ss.at[0, piece], recv_sem=f_rs.at[0, piece], device_id=device(12), device_id_type=MESH)

    def z_forward(piece):
        return pltpu.make_async_remote_copy(
            src_ref=relay_v.at[span(piece)], dst_ref=recv_v.at[1, span(piece)],
            send_sem=f_ss.at[1, piece], recv_sem=f_rs.at[1, piece],
            device_id=z_device(1 - piece % 2), device_id_type=MESH)

    def send(piece, _):
        x_copy(piece).start()
        z_copy(piece).start()
        core_copy(piece).start()
        return 0

    lax.fori_loop(0, PIECES, send, 0)

    for copy in bin_copies:
        copy.wait()
    own = jnp.concatenate([bins_ref[r] for r in range(ROUNDS)], axis=1)
    of_round = lax.broadcasted_iota(jnp.int32, (CB, 128), 1) // CB
    other = pbr_v[0]
    for r in range(1, ROUNDS):
        other = jnp.where(of_round == r, pbr_v[r], other)
    bin_ids = lax.broadcasted_iota(jnp.int32, (NB, 128), 0)
    for i in range(CB):
        one = (own[i : i + 1, :] == bin_ids).astype(F32)
        two = (other[i : i + 1, :] == bin_ids).astype(F32)
        oh_v[0, :, i * 128 : i * 128 + 128] = (one + two).astype(BF16)
        oh_v[1, :, i * 128 : i * 128 + 128] = (one - two).astype(BF16)

    mask = (
        lax.broadcasted_iota(jnp.int32, (FC, 256), 1) % FC == lax.broadcasted_iota(jnp.int32, (FC, 256), 0)
    ).astype(F32).astype(BF16)

    def products(q, _):
        start = (parity * CHUNKS + q) * CB
        parts = []
        for i in range(CB):
            v = [d_v[c, pl.ds(start + i, 8, stride=0), :] for c in range(2)]
            v = jnp.concatenate([jnp.concatenate([u, u], axis=0).astype(BF16) for u in v], axis=1)
            parts.append(v * mask)
        lhs = jnp.concatenate(parts, axis=0)
        other_part = recv_v[:, q].reshape(ROUNDS * CB, 256)
        turned = jnp.concatenate([-other_part[:, 128:], other_part[:, :128]], axis=1)
        rhs = jnp.concatenate([other_part, turned], axis=0)
        cross = nt_dot(lhs, rhs).astype(BF16)
        cross_v[:, pl.ds(pl.multiple_of(q * FC, FC), FC), :] = cross.reshape(CB, FC, 256)
        return 0

    def step(piece, _):
        @pl.when(piece < PIECES)
        def _():
            x_copy(piece).wait_recv()
            x_forward(piece).start()
            z_copy(piece).wait_recv()
            z_forward(piece).start()

        @pl.when(piece >= 1)
        def _():
            before = piece - 1
            core_copy(before).wait_recv()
            x_forward(before).wait_recv()
            z_forward(before).wait_recv()
            lax.fori_loop(before * CP, before * CP + CP, products, 0)
        return 0

    lax.fori_loop(0, PIECES + 1, step, 0)

    for c in range(2):
        for ft in range(HALF // 128):
            values = jnp.concatenate(
                [cross_v[i, ft * 128 : ft * 128 + 128, c * 128 : c * 128 + 128] for i in range(CB)], axis=1)
            total = nt_dot(oh_v[c], values)
            at = c * HALF + ft * 128
            part_v[:, :, at : at + 128] = total.astype(BF16).reshape(N_ROW, NB // N_ROW, 128)

    row_copies = [
        pltpu.make_async_remote_copy(
            src_ref=part_v.at[flip(row, k)], dst_ref=rows_v.at[k - 1],
            send_sem=row_ss.at[k - 1], recv_sem=row_rs.at[k - 1], device_id=device(16 * k), device_id_type=MESH)
        for k in range(1, N_ROW)
    ]
    for copy in row_copies:
        copy.start()
    total = part_v[row].astype(F32)
    for k, copy in enumerate(row_copies):
        copy.wait_recv()
        total = total + rows_v[k].astype(F32)
    for k in range(6):
        s2_v[pl.ds(k, N_COL, stride=8), :] = total[:, k * 128 : k * 128 + 128]

    col_copies = [
        pltpu.make_async_remote_copy(
            src_ref=s2_v.at[pl.ds(pl.multiple_of(flip(col, k) * 8, 8), 8), :], dst_ref=r2_v.at[k - 1],
            send_sem=col_ss.at[k - 1], recv_sem=col_rs.at[k - 1], device_id=device(k), device_id_type=MESH)
        for k in range(1, N_COL)
    ]
    for copy in col_copies:
        copy.start()
    load_e1.wait()
    load_e2.wait()
    sums = [s2_v[pl.ds(pl.multiple_of(col * 8, 8), 8), :], None]
    for k, copy in enumerate(col_copies, 1):
        copy.wait_recv()
        odd = bin(k).count("1") % 2
        sums[odd] = r2_v[k - 1] if sums[odd] is None else sums[odd] + r2_v[k - 1]

    result = None
    for which in range(2):
        half = parity if which == 0 else 1 - parity
        x = sums[which]
        reals, imags = [], []
        for ft in range(3):
            cos1 = e1_v[half, 0, :, ft * 128 : ft * 128 + 128]
            sin1 = e1_v[half, 1, :, ft * 128 : ft * 128 + 128]
            re, im = x[ft : ft + 1, :], x[3 + ft : 4 + ft, :]
            reals.append(re * cos1 - im * sin1)
            imags.append(re * sin1 + im * cos1)
        turned = jnp.concatenate(reals + imags, axis=1)
        high = turned.astype(BF16)
        low = (turned - high.astype(F32)).astype(BF16)
        both = jnp.concatenate([high, low], axis=0)
        for part in range(2):
            o = jnp.dot(both, e2_v[part, half], preferred_element_type=F32)
            o = o[:8] + o[8:]
            result = o if result is None else result + o
    for mh in range(LAGS // 128):
        out_ref[0:1, mh * 128 : mh * 128 + 128] = result[mh : mh + 1, :]

    for copy in row_copies + col_copies:
        copy.wait_send()

    def drain(piece, _):
        for make in (core_copy, x_copy, z_copy, x_forward, z_forward):
            make(piece).wait_send()
        return 0

    lax.fori_loop(0, PIECES, drain, 0)


def on_device(spectra, pair_bins, dead_mask):
    e1, e2 = tables()
    dma = pltpu.SemaphoreType.DMA
    return pl.pallas_call(
        kernel,
        out_shape=jax.ShapeDtypeStruct((1, LAGS), F32),
        in_specs=[
            pl.BlockSpec(memory_space=pltpu.SMEM),
            pl.BlockSpec(memory_space=pl.ANY),
            pl.BlockSpec(memory_space=pltpu.VMEM),
            pl.BlockSpec(memory_space=pl.ANY),
            pl.BlockSpec(memory_space=pl.ANY),
        ],
        out_specs=pl.BlockSpec(memory_space=pltpu.VMEM),
        scratch_shapes=[
            pltpu.VMEM((CB, W, 2 * F), BF16),
            pltpu.VMEM((2, 2 * CHUNKS * CB, 128), F32),
            pltpu.VMEM((CHUNKS, CB, 256), BF16),
            pltpu.VMEM((ROUNDS, CHUNKS, CB, 256), BF16),
            pltpu.VMEM((CHUNKS, CB, 256), BF16),
            pltpu.VMEM((CB, 128), jnp.int32),
            pltpu.VMEM((ROUNDS, CB, 128), jnp.int32),
            pltpu.VMEM((2, NB, CB * 128), BF16),
            pltpu.VMEM((CB, HALF, 256), BF16),
            pltpu.VMEM((N_ROW, NB // N_ROW, F), BF16),
            pltpu.VMEM((N_ROW - 1, NB // N_ROW, F), BF16),
            pltpu.VMEM((N_COL * 8, 128), F32),
            pltpu.VMEM((N_COL - 1, 8, 128), F32),
            pltpu.VMEM(e1.shape, F32),
            pltpu.VMEM(e2.shape, BF16),
            dma((3,)), dma((ROUNDS,)), dma((ROUNDS,)),
            dma((3, PIECES)), dma((3, PIECES)), dma((2, PIECES)), dma((2, PIECES)),
            dma((N_ROW - 1,)), dma((N_ROW - 1,)), dma((N_COL - 1,)), dma((N_COL - 1,)),
        ],
        compiler_params=pltpu.CompilerParams(
            collective_id=0, has_side_effects=True, vmem_limit_bytes=48 << 20),
        name="correlate",
    )(dead_mask, spectra, pair_bins, jnp.asarray(e1), jnp.asarray(e2))


def solution(mesh):
    return jax.shard_map(
        on_device,
        mesh=mesh,
        in_specs=(P(("row", "col"), None, None), P(None, ("row", "col"), None), P(("row", "col"))),
        out_specs=P(("row", "col"), None),
        check_vma=False,
    )
```

time: 458 us -> 54.2 us (0.12); the launches traced: 453 us -> 54 us
  matrix products: 135 us -> 0 us
  local copies, waits for them, and re-layouts: 139 us -> 5.14 us
  waiting for transfers between devices: 131 us -> 0 us
  Pallas kernels: 0 us -> 48.8 us
  other arithmetic: 25.4 us -> 0 us
  between operations: 13.9 us -> 0.01 us
  starting transfers between devices: 8.76 us -> 0 us
    dot_general x21 -> x0, matrix products: 135 us -> none  [the longest x4 35 us: cross_spectra(): jnp.einsum('iwk,jwk->ijk', one_real, two_real, preferred_element_type=jnp...]
    unnamed x2 -> x0, waiting for transfers between devices: 131 us -> none
    sub x4 -> x0, local copies, waits for them, and re-layouts: 56.3 us -> none  [cross_spectra(): jnp.einsum('iwk,jwk->ijk', one_imag, two_real, preferred_element_type=jnp...]
    pallas_call x0 -> x1, Pallas kernels: none -> 48.8 us  [on_device(): pl.pallas_call(kernel, out_shape=jax.ShapeDtypeStruct((1, LAGS), F32), in...]
    add x4 -> x0, local copies, waits for them, and re-layouts: 44.5 us -> none  [cross_spectra(): jnp.einsum('iwk,jwk->ijk', one_real, two_real, preferred_element_type=jnp...]
    unnamed x44 -> x11, local copies, waits for them, and re-layouts: 23.2 us -> 5.14 us
    mul x2 -> x0, other arithmetic: 12.6 us -> none  [the longest x1 12.6 us: build_table(): weights * jnp.cos(angles)]
    slice x8 -> x0, local copies, waits for them, and re-layouts: 12.4 us -> none  [the longest x4 8.09 us: cross_spectra(): remote_part[..., :half_len]]
  transfers between devices with their start and end apart: 5 -> 0, of which waited for: 1 -> 0; matrix products, arithmetic and copies ran while one was open for 16% -> 0% of each run, Pallas kernels for 0% -> 0%
where the time goes in v1:
time: 54.2 us; the launch traced here: 54 us
  Pallas kernels  48.8 us (90%)
  local copies, waits for them, and re-layouts  5.14 us (9%)
    pallas_call x1, Pallas kernels, on_device(): pl.pallas_call(kernel, out_shape=jax.ShapeDtypeStruct((1, LAGS), F32), in...  48.8 us
    unnamed x11, local copies, waits for them, and re-layouts  5.14 us

profile of v1, /device:TPU:1, one launch (start us, length us, event | category | flops | bytes accessed | tf_op | source)
XLA Modules:
  0.0 54.0 jit_solution(11501874534414195440)
XLA Ops:
  0.0 0.0 copy-start
  0.0 1.1 %copy-done = bf16[32,8,1536]{2,1,0:T(8,128)(2,1)S(1)} copy-done((bf16[32,8,1536]{2,1,0:T(8,128)(2,1)S(1)}, bf16[32,8,1536]{2,1,0:T(8,128)(2,1)}, u32[]{:S(2)}) %copy-start) | copy-done | bytes 786456
  1.1 0.0 copy-start.1
  1.1 1.1 %copy-done.1 = bf16[2,2,768,128]{3,2,1,0:T(8,128)(2,1)S(1)} copy-done((bf16[2,2,768,128]{3,2,1,0:T(8,128)(2,1)S(1)}, bf16[2,2,768,128]{3,2,1,0:T(8,128)(2,1)}, u32[]{:S(2)}) %copy-start.1) | copy-done | bytes 786456
  2.3 0.0 copy-start.2
  2.3 0.8 %copy-done.2 = s32[4,32,32]{2,1,0:T(8,128)S(1)} copy-done((s32[4,32,32]{2,1,0:T(8,128)S(1)}, s32[4,32,32]{2,1,0:T(8,128)}, u32[]{:S(2)}) %copy-start.2) | copy-done | bytes 16408
  3.1 0.0 copy-start.3
  3.1 0.8 %copy-done.3 = f32[2,2,8,384]{3,2,1,0:T(8,128)S(1)} copy-done((f32[2,2,8,384]{3,2,1,0:T(8,128)S(1)}, f32[2,2,8,384]{3,2,1,0:T(8,128)}, u32[]{:S(2)}) %copy-start.3) | copy-done | bytes 49176
  3.9 0.0 copy-start.4
  3.9 0.7 %copy-done.4 = s32[32]{0:T(128)S(1)} copy-done((s32[32]{0:T(128)S(1)}, s32[32]{0:T(128)}, u32[]{:S(2)}) %copy-start.4) | copy-done | bytes 152
  4.6 48.8 %correlate.1 = f32[1,896]{1,0:T(1,128)S(1)} custom-call(s32[32]{0:T(128)S(1)} %copy-done.4, bf16[32,8,1536]{2,1,0:T(8,128)(2,1)S(1)} %copy-done, s32[4,32,32]{2,1,0:T(8,128)S(1)} %copy-done.2, f32[2,2,8,384]{3,2,1,0:T(8,128)S(1)} %copy-done.3, bf16[2,2,768,128]{3,2,1,0:T(8,128)(2,1)S(1)} %copy-done.1), custom_call_target="tpu_custom_call" | custom-call | tf_op jit(solution)/shard_map/correlate/pallas_call | solution.py:296
  53.4 0.6 %copy.7 = f32[1,896]{1,0:T(1,128)} copy(f32[1,896]{1,0:T(1,128)S(1)} %correlate.1) | data formatting | bytes 7168
Async XLA Ops:
  0.0 1.1 %copy-start = (bf16[32,8,1536]{2,1,0:T(8,128)(2,1)S(1)}, bf16[32,8,1536]{2,1,0:T(8,128)(2,1)}, u32[]{:S(2)}) copy-start(bf16[32,8,1536]{2,1,0:T(8,128)(2,1)} %spec_hbm.1) | copy-start | bytes 2359300
  1.1 1.1 %copy-start.1 = (bf16[2,2,768,128]{3,2,1,0:T(8,128)(2,1)S(1)}, bf16[2,2,768,128]{3,2,1,0:T(8,128)(2,1)}, u32[]{:S(2)}) copy-start(bf16[2,2,768,128]{3,2,1,0:T(8,128)(2,1)} %constant.5.clone.e2_hbm) | copy-start | bytes 2359300
  2.3 0.8 %copy-start.2 = (s32[4,32,32]{2,1,0:T(8,128)S(1)}, s32[4,32,32]{2,1,0:T(8,128)}, u32[]{:S(2)}) copy-start(s32[4,32,32]{2,1,0:T(8,128)} %bins_ref.1) | copy-start | bytes 49156
  3.1 0.8 %copy-start.3 = (f32[2,2,8,384]{3,2,1,0:T(8,128)S(1)}, f32[2,2,8,384]{3,2,1,0:T(8,128)}, u32[]{:S(2)}) copy-start(f32[2,2,8,384]{3,2,1,0:T(8,128)} %constant.4.clone.e1_hbm) | copy-start | bytes 147460
  3.9 0.7 %copy-start.4 = (s32[32]{0:T(128)S(1)}, s32[32]{0:T(128)}, u32[]{:S(2)}) copy-start(s32[32]{0:T(128)} %alive_ref.1) | copy-start | bytes 388

commit v2 on v1

v2 whole, which is shorter than its diff:
```python
import functools
import math

import jax
import jax.numpy as jnp
import numpy as np
from jax import lax
from jax.experimental import pallas as pl
from jax.experimental.pallas import tpu as pltpu
from jax.sharding import PartitionSpec as P

NT = 1600
LAGS = 896
NB = 128
ROUNDS = 4
CB = 32
W = 8
F = 768
N_ROW = 8
N_COL = 16
FC = 16
HALF = F // 2
CHUNKS = HALF // FC
PIECES = 6
CP = CHUNKS // PIECES
LAG = 3
GROUPS = HALF // 128
MESH = pl.DeviceIdType.MESH
F32 = jnp.float32
BF16 = jnp.bfloat16


def tables():
    at = np.arange(F, dtype=np.int64)
    k = at // 128 * 128 + -(at % 128 // FC) % 8 * FC + at % FC
    scale = 1.0 / (2.0 * math.sqrt(F * W * (ROUNDS * CB * CB * N_ROW * N_COL // NB)))
    weight = np.where(k == 0, 1.0, 2.0) * scale
    start = 128 * np.arange(8, dtype=np.int64) - LAGS // 2
    first = (start[:, None] * k[None, :] % NT) * (2.0 * np.pi / NT)
    cos1 = (np.cos(first) * weight).reshape(8, 2, HALF).transpose(1, 0, 2)
    sin1 = (np.sin(first) * weight).reshape(8, 2, HALF).transpose(1, 0, 2)
    e1 = np.stack([cos1, sin1], axis=1).astype(np.float32)
    second = (k[:, None] * np.arange(128, dtype=np.int64)[None, :] % NT) * (2.0 * np.pi / NT)
    cos2 = np.cos(second).reshape(2, HALF, 128)
    sin2 = -np.sin(second).reshape(2, HALF, 128)
    e2 = np.concatenate([cos2, sin2], axis=1).astype(np.float32)
    high = e2.astype(jnp.bfloat16)
    low = (e2 - high.astype(np.float32)).astype(jnp.bfloat16)
    return e1, np.stack([high, low], axis=0)


def flip(value, mask):
    for bit in range(4):
        if mask >> bit & 1:
            value = value + (1 << bit) * (1 - 2 * ((value // (1 << bit)) % 2))
    return value


def nt_dot(a, b):
    return lax.dot_general(a, b, (((1,), (1,)), ((), ())), preferred_element_type=F32)


def kernel(
    alive_hbm, spec_hbm, bins_hbm, e1_hbm, e2_hbm, out_ref,
    alive_ref, bins_ref, scale_v, x_v, d_v, send_v, recv_v, pbs_v, pbr_v, oh_v, cross_v, part_v, rows_v, s2_v, r2_v, e1_v, e2_v,
    local_sem, pb_ss, pb_rs, a_ss, a_rs, f_ss, f_rs, row_ss, row_rs, col_ss, col_rs,
):
    row = lax.axis_index("row")
    col = lax.axis_index("col")
    parity = (col + col // 2 + col // 4 + col // 8) % 2

    def device(mask):
        return (flip(row, mask >> 4), flip(col, mask & 15))

    loads = [
        pltpu.make_async_copy(source, target, local_sem.at[n])
        for n, (source, target) in enumerate([
            (bins_hbm, bins_ref), (alive_hbm, alive_ref), (spec_hbm, x_v), (e1_hbm, e1_v), (e2_hbm, e2_v)])
    ]
    for load in loads:
        load.start()

    peers = sorted({16 * k for k in range(1, N_ROW)} | set(range(1, N_COL)))
    barrier = pltpu.get_barrier_semaphore()
    for mask in peers:
        pl.semaphore_signal(barrier, inc=1, device_id=device(mask), device_id_type=MESH)

    loads[0].wait()
    bins = bins_ref[...].reshape(ROUNDS * CB, CB)
    padded = jnp.concatenate([bins, jnp.zeros((128, 96), jnp.int32)], axis=1).astype(F32)
    pbs_v[...] = padded.T[:CB, :].astype(jnp.int32)
    loads[1].wait()
    loads[2].wait()

    def scales(i, _):
        x = x_v[i].astype(F32)
        power = jnp.mean(x * x, axis=-1, keepdims=True)
        alive = alive_ref[i].astype(F32)
        scale_v[i] = jnp.broadcast_to(alive / jnp.sqrt(power + 1e-06), (W, 128))
        return 0

    lax.fori_loop(0, CB, scales, 0, unroll=8)

    lane = lax.broadcasted_iota(jnp.int32, (8, 128), 1) // 16
    bits = [(lane // (1 << s)) % 2 == 1 for s in range(3)]

    def whiten(ft):
        def one(i, _):
            for c in range(2):
                at = pl.multiple_of(c * F + ft * 128, 128)
                t = x_v[i, :, pl.ds(at, 128)].astype(F32) * scale_v[i]
                t = pltpu.roll(t, 0, 1, stride=16, stride_axis=0)
                for s in range(3):
                    t = jnp.where(bits[s], pltpu.roll(t, 8 - (1 << s), 0), t)
                d_v[c, pl.ds(ft * 8 * CB + i, 8, stride=CB), :] = t
            return 0

        lax.fori_loop(0, CB, one, 0, unroll=8)

    def span(piece):
        return pl.ds(piece * CP, CP)

    def core_copy(piece):
        return pltpu.make_async_remote_copy(
            src_ref=send_v.at[span(piece)], dst_ref=recv_v.at[0, span(piece)],
            send_sem=a_ss.at[0, piece], recv_sem=a_rs.at[0, piece], device_id=device(1), device_id_type=MESH)

    def x_copy(piece):
        return pltpu.make_async_remote_copy(
            src_ref=send_v.at[span(piece)], dst_ref=recv_v.at[2, span(piece)],
            send_sem=a_ss.at[1, piece], recv_sem=a_rs.at[1, piece], device_id=device(4), device_id_type=MESH)

    def z_copy(piece):
        return pltpu.make_async_remote_copy(
            src_ref=send_v.at[span(piece)], dst_ref=recv_v.at[1, span(piece)],
            send_sem=a_ss.at[2, piece], recv_sem=a_rs.at[2, piece], device_id=device(2), device_id_type=MESH)

    def x_forward(piece):
        return pltpu.make_async_remote_copy(
            src_ref=recv_v.at[2, span(piece)], dst_ref=recv_v.at[3, span(piece)],
            send_sem=f_ss.at[piece], recv_sem=f_rs.at[piece], device_id=device(12), device_id_type=MESH)

    bin_copies = [
        pltpu.make_async_remote_copy(
            src_ref=pbs_v, dst_ref=pbr_v.at[r], send_sem=pb_ss.at[r], recv_sem=pb_rs.at[r],
            device_id=device(1 << r), device_id_type=MESH)
        for r in range(ROUNDS)
    ]

    def send(group, _):
        whiten((1 - parity) * GROUPS + group)

        def pack(k, _):
            q = group * 8 + k
            start = pl.multiple_of(((1 - parity) * CHUNKS + q) * CB, CB)
            for c in range(2):
                send_v[q, :, c * 128 : c * 128 + 128] = d_v[c, pl.ds(start, CB), :].astype(BF16)
            return 0

        lax.fori_loop(0, 8, pack, 0, unroll=2)

        @pl.when(group == 0)
        def _():
            pl.semaphore_wait(barrier, len(peers))
            for copy in bin_copies:
                copy.start()

        def start(piece, _):
            x_copy(piece).start()
            z_copy(piece).start()
            core_copy(piece).start()
            return 0

        lax.fori_loop(group * (8 // CP), (group + 1) * (8 // CP), start, 0)
        return 0

    lax.fori_loop(0, GROUPS, send, 0)

    def rest(group, _):
        whiten(parity * GROUPS + group)
        return 0

    lax.fori_loop(0, GROUPS, rest, 0)

    def forward(piece):
        x_copy(piece).wait_recv()
        x_forward(piece).start()

    forward(0)
    for copy in bin_copies:
        copy.wait()
    own = jnp.concatenate([bins_ref[r] for r in range(ROUNDS)], axis=1)
    of_round = lax.broadcasted_iota(jnp.int32, (CB, 128), 1) // CB
    other = pbr_v[0]
    for r in range(1, ROUNDS):
        other = jnp.where(of_round == r, pbr_v[r], other)
    bin_ids = lax.broadcasted_iota(jnp.int32, (NB, 128), 0)
    for i in range(CB):
        one = (own[i : i + 1, :] == bin_ids).astype(F32)
        two = (other[i : i + 1, :] == bin_ids).astype(F32)
        oh_v[0, :, i * 128 : i * 128 + 128] = (one + two).astype(BF16)
        oh_v[1, :, i * 128 : i * 128 + 128] = (one - two).astype(BF16)

    forward(1)
    forward(2)

    mask = (
        lax.broadcasted_iota(jnp.int32, (FC, 256), 1) % FC == lax.broadcasted_iota(jnp.int32, (FC, 256), 0)
    ).astype(F32).astype(BF16)

    def products(q, _):
        start = (parity * CHUNKS + q) * CB
        parts = []
        for i in range(CB):
            v = [d_v[c, pl.ds(start + i, 8, stride=0), :] for c in range(2)]
            v = jnp.concatenate([jnp.concatenate([u, u], axis=0).astype(BF16) for u in v], axis=1)
            parts.append(v * mask)
        lhs = jnp.concatenate(parts, axis=0)
        other_part = recv_v[:, q].reshape(ROUNDS * CB, 256)
        turned = jnp.concatenate([-other_part[:, 128:], other_part[:, :128]], axis=1)
        rhs = jnp.concatenate([other_part, turned], axis=0)
        cross = nt_dot(lhs, rhs).astype(BF16)
        cross_v[:, pl.ds(pl.multiple_of(q * FC, FC), FC), :] = cross.reshape(CB, FC, 256)
        return 0

    def row_copy(g, k):
        return pltpu.make_async_remote_copy(
            src_ref=part_v.at[g, flip(row, k)], dst_ref=rows_v.at[g, k - 1],
            send_sem=row_ss.at[g, k - 1], recv_sem=row_rs.at[g, k - 1],
            device_id=device(16 * k), device_id_type=MESH)

    def stack(g):
        for c in range(2):
            at = pl.ds(pl.multiple_of(g * 128, 128), 128)
            values = jnp.concatenate([cross_v[i, at, c * 128 : c * 128 + 128] for i in range(CB)], axis=1)
            total = nt_dot(oh_v[c], values)
            part_v[g, :, :, c * 128 : c * 128 + 128] = total.astype(BF16).reshape(N_ROW, NB // N_ROW, 128)
        for k in range(1, N_ROW):
            row_copy(g, k).start()

    def step(piece, _):
        @pl.when(piece < PIECES)
        def _():
            forward(piece)

        before = piece - LAG
        core_copy(before).wait_recv()
        z_copy(before).wait_recv()
        x_forward(before).wait_recv()
        lax.fori_loop(0, CP, lambda k, _: products(before * CP + k, _), 0, unroll=CP)

        @pl.when(before % 2 == 1)
        def _():
            stack(before // 2)
        return 0

    lax.fori_loop(LAG, PIECES + LAG, step, 0)

    for g in range(GROUPS):
        total = part_v[g, row].astype(F32)
        for k in range(1, N_ROW):
            row_copy(g, k).wait_recv()
            total = total + rows_v[g, k - 1].astype(F32)
        for c in range(2):
            s2_v[pl.ds(c * GROUPS + g, N_COL, stride=8), :] = total[:, c * 128 : c * 128 + 128]

    col_copies = [
        pltpu.make_async_remote_copy(
            src_ref=s2_v.at[pl.ds(pl.multiple_of(flip(col, k) * 8, 8), 8), :], dst_ref=r2_v.at[k - 1],
            send_sem=col_ss.at[k - 1], recv_sem=col_rs.at[k - 1], device_id=device(k), device_id_type=MESH)
        for k in range(1, N_COL)
    ]
    for copy in col_copies:
        copy.start()
    loads[3].wait()
    loads[4].wait()
    sums = [s2_v[pl.ds(pl.multiple_of(col * 8, 8), 8), :], None]
    for k, copy in enumerate(col_copies, 1):
        copy.wait_recv()
        odd = bin(k).count("1") % 2
        sums[odd] = r2_v[k - 1] if sums[odd] is None else sums[odd] + r2_v[k - 1]

    result = None
    for which in range(2):
        half = parity if which == 0 else 1 - parity
        x = sums[which]
        reals, imags = [], []
        for ft in range(3):
            cos1 = e1_v[half, 0, :, ft * 128 : ft * 128 + 128]
            sin1 = e1_v[half, 1, :, ft * 128 : ft * 128 + 128]
            re, im = x[ft : ft + 1, :], x[3 + ft : 4 + ft, :]
            reals.append(re * cos1 - im * sin1)
            imags.append(re * sin1 + im * cos1)
        turned = jnp.concatenate(reals + imags, axis=1)
        high = turned.astype(BF16)
        low = (turned - high.astype(F32)).astype(BF16)
        both = jnp.concatenate([high, low], axis=0)
        for part in range(2):
            o = jnp.dot(both, e2_v[part, half], preferred_element_type=F32)
            o = o[:8] + o[8:]
            result = o if result is None else result + o
    for mh in range(LAGS // 128):
        out_ref[0:1, mh * 128 : mh * 128 + 128] = result[mh : mh + 1, :]

    for copy in col_copies:
        copy.wait_send()
    for g in range(GROUPS):
        for k in range(1, N_ROW):
            row_copy(g, k).wait_send()

    def drain(piece, _):
        for make in (core_copy, x_copy, z_copy, x_forward):
            make(piece).wait_send()
        return 0

    lax.fori_loop(0, PIECES, drain, 0)


def on_device(spectra, pair_bins, dead_mask):
    e1, e2 = tables()
    dma = pltpu.SemaphoreType.DMA
    return pl.pallas_call(
        kernel,
        out_shape=jax.ShapeDtypeStruct((1, LAGS), F32),
        in_specs=[pl.BlockSpec(memory_space=pl.ANY)] * 5,
        out_specs=pl.BlockSpec(memory_space=pltpu.VMEM),
        scratch_shapes=[
            pltpu.SMEM((CB,), jnp.int32),
            pltpu.VMEM((ROUNDS, CB, CB), jnp.int32),
            pltpu.VMEM((CB, W, 128), F32),
            pltpu.VMEM((CB, W, 2 * F), BF16),
            pltpu.VMEM((2, 2 * CHUNKS * CB, 128), F32),
            pltpu.VMEM((CHUNKS, CB, 256), BF16),
            pltpu.VMEM((ROUNDS, CHUNKS, CB, 256), BF16),
            pltpu.VMEM((CB, 128), jnp.int32),
            pltpu.VMEM((ROUNDS, CB, 128), jnp.int32),
            pltpu.VMEM((2, NB, CB * 128), BF16),
            pltpu.VMEM((CB, HALF, 256), BF16),
            pltpu.VMEM((GROUPS, N_ROW, NB // N_ROW, 256), BF16),
            pltpu.VMEM((GROUPS, N_ROW - 1, NB // N_ROW, 256), BF16),
            pltpu.VMEM((N_COL * 8, 128), F32),
            pltpu.VMEM((N_COL - 1, 8, 128), F32),
            pltpu.VMEM(e1.shape, F32),
            pltpu.VMEM(e2.shape, BF16),
            dma((5,)), dma((ROUNDS,)), dma((ROUNDS,)),
            dma((3, PIECES)), dma((3, PIECES)), dma((PIECES,)), dma((PIECES,)),
            dma((GROUPS, N_ROW - 1)), dma((GROUPS, N_ROW - 1)), dma((N_COL - 1,)), dma((N_COL - 1,)),
        ],
        compiler_params=pltpu.CompilerParams(
            collective_id=0, has_side_effects=True, vmem_limit_bytes=64 << 20),
        name="correlate",
    )(dead_mask, spectra, pair_bins, jnp.asarray(e1), jnp.asarray(e2))


def solution(mesh):
    return jax.shard_map(
        on_device,
        mesh=mesh,
        in_specs=(P(("row", "col"), None, None), P(None, ("row", "col"), None), P(("row", "col"))),
        out_specs=P(("row", "col"), None),
        check_vma=False,
    )
```

time: 54.2 us -> 37.3 us (0.69)
  Pallas kernels: 48.8 us -> 35.9 us
  local copies, waits for them, and re-layouts: 5.14 us -> 1.26 us
    pallas_call x1, Pallas kernels: 48.8 us -> 35.9 us  [on_device(): pl.pallas_call(kernel, out_shape=jax.ShapeDtypeStruct((1, LAGS), F32), in...]
    unnamed x11 -> x1, local copies, waits for them, and re-layouts: 5.14 us -> 1.26 us
where the time goes in v2:
time: 37.3 us; the launch traced here: 37.1 us
  Pallas kernels  35.9 us (96%)
  local copies, waits for them, and re-layouts  1.26 us (3%)
    pallas_call x1, Pallas kernels, on_device(): pl.pallas_call(kernel, out_shape=jax.ShapeDtypeStruct((1, LAGS), F32), in...  35.9 us
    unnamed x1, local copies, waits for them, and re-layouts  1.26 us

profile of v2, /device:TPU:1, one launch (start us, length us, event | category | flops | bytes accessed | tf_op | source)
XLA Modules:
  0.0 37.1 jit_solution(9576488511706466149)
XLA Ops:
  0.0 35.9 %correlate.1 = f32[1,896]{1,0:T(1,128)} custom-call(s32[32]{0:T(128)} %alive_hbm.1, bf16[32,8,1536]{2,1,0:T(8,128)(2,1)} %spec_hbm.1, s32[4,32,32]{2,1,0:T(8,128)} %bins_hbm.1, f32[2,2,8,384]{3,2,1,0:T(8,128)} %constant.4.clone.e1_hbm, bf16[2,2,768,128]{3,2,1,0:T(8,128)(2,1)} %constant.5.clone.e2_hbm), custom_call_target="tpu_custom_call" | custom-call | tf_op jit(solution)/shard_map/correlate/pallas_call | solution.py:322
  35.9 1.3 %copy.7 = f32[1,896]{1,0:T(1,128)} copy(f32[1,896]{1,0:T(1,128)} %correlate.1) | data formatting | bytes 7168

commit v3 on v2

--- a/solution.py
+++ b/solution.py
@@ -23,8 +23,11 @@
 CHUNKS = HALF // FC
 PIECES = 6
 CP = CHUNKS // PIECES
-LAG = 3
+LAG = 4
 GROUPS = HALF // 128
+NEAR = 8
+FAR = 16
+STACKS = ((0, 256), (256, 128))
 MESH = pl.DeviceIdType.MESH
 F32 = jnp.float32
 BF16 = jnp.bfloat16
@@ -56,17 +59,26 @@
     return value
 
 
+def links(mask):
+    steps = (0, 1, 2, 1)
+    x, y, z = mask >> 2 & 3, mask >> 5 & 3, (mask >> 4 & 1) + (mask & 2)
+    return steps[x] + steps[y] + steps[z]
+
+
 def nt_dot(a, b):
     return lax.dot_general(a, b, (((1,), (1,)), ((), ())), preferred_element_type=F32)
 
 
 def kernel(
     alive_hbm, spec_hbm, bins_hbm, e1_hbm, e2_hbm, out_ref,
-    alive_ref, bins_ref, scale_v, x_v, d_v, send_v, recv_v, pbs_v, pbr_v, oh_v, cross_v, part_v, rows_v, s2_v, r2_v, e1_v, e2_v,
-    local_sem, pb_ss, pb_rs, a_ss, a_rs, f_ss, f_rs, row_ss, row_rs, col_ss, col_rs,
+    alive_ref, bins_ref, scale_v, x_v, d_v, send_v, recv_v, pbs_v, pbr_v, oh_v, cross_v, part0_v, part1_v, near0_v, near1_v, s2_v, r2_v, e1_v, e2_v,
+    local_sem, pb_ss, pb_rs, a_ss, a_rs, f_ss, f_rs, near_ss, near_rs, far_ss, far_rs, entered,
 ):
+    parts, nears = (part0_v, part1_v), (near0_v, near1_v)
     row = lax.axis_index("row")
     col = lax.axis_index("col")
+    near = col // 4 * 2 + col % 2
+    far = row * 2 + col // 2 % 2
     parity = (col + col // 2 + col // 4 + col // 8) % 2
 
     def device(mask):
@@ -80,7 +92,7 @@
     for load in loads:
         load.start()
 
-    peers = sorted({16 * k for k in range(1, N_ROW)} | set(range(1, N_COL)))
+    peers = sorted([1, 4, 5, 8, 9, 12, 13, 2, 16, 18, 32, 64, 96], key=links, reverse=True)
     barrier = pltpu.get_barrier_semaphore()
     for mask in peers:
         pl.semaphore_signal(barrier, inc=1, device_id=device(mask), device_id_type=MESH)
@@ -165,13 +177,15 @@
             for copy in bin_copies:
                 copy.start()
 
-        def start(piece, _):
-            x_copy(piece).start()
-            z_copy(piece).start()
-            core_copy(piece).start()
-            return 0
-
-        lax.fori_loop(group * (8 // CP), (group + 1) * (8 // CP), start, 0)
+        pieces = [group * (8 // CP) + k for k in range(8 // CP)]
+        for piece in pieces:
+            for make in (x_copy, z_copy, core_copy):
+                make(piece).start()
+
+        @pl.when(group == 0)
+        def _():
+            for along_z in (2, 16, 18):
+                pl.semaphore_signal(entered, inc=1, device_id=device(along_z), device_id_type=MESH)
         return 0
 
     lax.fori_loop(0, GROUPS, send, 0)
@@ -187,6 +201,7 @@
         x_forward(piece).start()
 
     forward(0)
+    forward(1)
     for copy in bin_copies:
         copy.wait()
     own = jnp.concatenate([bins_ref[r] for r in range(ROUNDS)], axis=1)
@@ -194,15 +209,16 @@
     other = pbr_v[0]
     for r in range(1, ROUNDS):
         other = jnp.where(of_round == r, pbr_v[r], other)
-    bin_ids = lax.broadcasted_iota(jnp.int32, (NB, 128), 0)
+    place = lax.broadcasted_iota(jnp.int32, (NB, 128), 0)
+    bin_ids = place // 2 % 8 * 16 + place // 32 * 4 + place % 2 * 2 + place // 16 % 2
     for i in range(CB):
         one = (own[i : i + 1, :] == bin_ids).astype(F32)
         two = (other[i : i + 1, :] == bin_ids).astype(F32)
         oh_v[0, :, i * 128 : i * 128 + 128] = (one + two).astype(BF16)
         oh_v[1, :, i * 128 : i * 128 + 128] = (one - two).astype(BF16)
 
-    forward(1)
-    forward(2)
+    for k in range(2, LAG):
+        forward(k)
 
     mask = (
         lax.broadcasted_iota(jnp.int32, (FC, 256), 1) % FC == lax.broadcasted_iota(jnp.int32, (FC, 256), 0)
@@ -223,20 +239,26 @@
         cross_v[:, pl.ds(pl.multiple_of(q * FC, FC), FC), :] = cross.reshape(CB, FC, 256)
         return 0
 
-    def row_copy(g, k):
-        return pltpu.make_async_remote_copy(
-            src_ref=part_v.at[g, flip(row, k)], dst_ref=rows_v.at[g, k - 1],
-            send_sem=row_ss.at[g, k - 1], recv_sem=row_rs.at[g, k - 1],
-            device_id=device(16 * k), device_id_type=MESH)
+    near_mask = [k // 2 * 4 + k % 2 for k in range(NEAR)]
+    far_mask = [k // 2 * 16 + k % 2 * 2 for k in range(FAR)]
+    near_order = sorted(range(1, NEAR), key=lambda k: -links(near_mask[k]))
+    far_order = sorted(range(1, FAR), key=lambda k: -links(far_mask[k]))
+
+    def near_copy(g, k):
+        return pltpu.make_async_remote_copy(
+            src_ref=parts[g].at[flip(near, k)], dst_ref=nears[g].at[k - 1],
+            send_sem=near_ss.at[g, k - 1], recv_sem=near_rs.at[g, k - 1],
+            device_id=device(near_mask[k]), device_id_type=MESH)
 
     def stack(g):
+        first, count = STACKS[g]
         for c in range(2):
-            at = pl.ds(pl.multiple_of(g * 128, 128), 128)
-            values = jnp.concatenate([cross_v[i, at, c * 128 : c * 128 + 128] for i in range(CB)], axis=1)
+            values = jnp.concatenate(
+                [cross_v[i, first : first + count, c * 128 : c * 128 + 128] for i in range(CB)], axis=1)
             total = nt_dot(oh_v[c], values)
-            part_v[g, :, :, c * 128 : c * 128 + 128] = total.astype(BF16).reshape(N_ROW, NB // N_ROW, 128)
-        for k in range(1, N_ROW):
-            row_copy(g, k).start()
+            parts[g][:, :, c * count : c * count + count] = total.astype(BF16).reshape(NEAR, FAR, count)
+        for k in near_order:
+            near_copy(g, k).start()
 
     def step(piece, _):
         @pl.when(piece < PIECES)
@@ -249,41 +271,59 @@
         x_forward(before).wait_recv()
         lax.fori_loop(0, CP, lambda k, _: products(before * CP + k, _), 0, unroll=CP)
 
-        @pl.when(before % 2 == 1)
-        def _():
-            stack(before // 2)
+        for g, (first, count) in enumerate(STACKS):
+            @pl.when(before == (first + count) // (FC * CP) - 1)
+            def _():
+                stack(g)
         return 0
 
     lax.fori_loop(LAG, PIECES + LAG, step, 0)
 
-    for g in range(GROUPS):
-        total = part_v[g, row].astype(F32)
-        for k in range(1, N_ROW):
-            row_copy(g, k).wait_recv()
-            total = total + rows_v[g, k - 1].astype(F32)
-        for c in range(2):
-            s2_v[pl.ds(c * GROUPS + g, N_COL, stride=8), :] = total[:, c * 128 : c * 128 + 128]
-
-    col_copies = [
+    def drain(piece, _):
+        for make in (core_copy, x_copy, z_copy, x_forward):
+            make(piece).wait_send()
+        return 0
+
+    lax.fori_loop(0, PIECES, drain, 0)
+
+    for g, (first, count) in enumerate(STACKS):
+        totals = [parts[g][near].astype(F32), None]
+        for k in range(1, NEAR):
+            near_copy(g, k).wait_recv()
+            value = nears[g][k - 1].astype(F32)
+            odd = bin(near_mask[k]).count("1") % 2
+            totals[odd] = value if totals[odd] is None else totals[odd] + value
+        for odd in range(2):
+            half = parity if odd == 0 else 1 - parity
+            for c in range(2):
+                for n in range(count // 128):
+                    at = half * 8 + c * GROUPS + first // 128 + n
+                    value = totals[odd][:, c * count + n * 128 : c * count + n * 128 + 128]
+                    s2_v[pl.ds(at, FAR, stride=16), :] = value
+
+    far_copies = [
         pltpu.make_async_remote_copy(
-            src_ref=s2_v.at[pl.ds(pl.multiple_of(flip(col, k) * 8, 8), 8), :], dst_ref=r2_v.at[k - 1],
-            send_sem=col_ss.at[k - 1], recv_sem=col_rs.at[k - 1], device_id=device(k), device_id_type=MESH)
-        for k in range(1, N_COL)
+            src_ref=s2_v.at[pl.ds(pl.multiple_of(flip(far, k) * 16, 16), 16), :], dst_ref=r2_v.at[k - 1],
+            send_sem=far_ss.at[k - 1], recv_sem=far_rs.at[k - 1],
+            device_id=device(far_mask[k]), device_id_type=MESH)
+        for k in far_order
     ]
-    for copy in col_copies:
+    pl.semaphore_wait(entered, 3)
+    for copy in far_copies:
         copy.start()
+    for g in range(len(STACKS)):
+        for k in range(1, NEAR):
+            near_copy(g, k).wait_send()
     loads[3].wait()
     loads[4].wait()
-    sums = [s2_v[pl.ds(pl.multiple_of(col * 8, 8), 8), :], None]
-    for k, copy in enumerate(col_copies, 1):
+    sums = s2_v[pl.ds(pl.multiple_of(far * 16, 16), 16), :]
+    for k, copy in zip(far_order, far_copies):
         copy.wait_recv()
-        odd = bin(k).count("1") % 2
-        sums[odd] = r2_v[k - 1] if sums[odd] is None else sums[odd] + r2_v[k - 1]
+        sums = sums + r2_v[k - 1]
 
     result = None
-    for which in range(2):
-        half = parity if which == 0 else 1 - parity
-        x = sums[which]
+    for half in range(2):
+        x = sums[half * 8 : half * 8 + 8]
         reals, imags = [], []
         for ft in range(3):
             cos1 = e1_v[half, 0, :, ft * 128 : ft * 128 + 128]
@@ -302,18 +342,8 @@
     for mh in range(LAGS // 128):
         out_ref[0:1, mh * 128 : mh * 128 + 128] = result[mh : mh + 1, :]
 
-    for copy in col_copies:
+    for copy in far_copies:
         copy.wait_send()
-    for g in range(GROUPS):
-        for k in range(1, N_ROW):
-            row_copy(g, k).wait_send()
-
-    def drain(piece, _):
-        for make in (core_copy, x_copy, z_copy, x_forward):
-            make(piece).wait_send()
-        return 0
-
-    lax.fori_loop(0, PIECES, drain, 0)
 
 
 def on_device(spectra, pair_bins, dead_mask):
@@ -336,20 +366,24 @@
             pltpu.VMEM((ROUNDS, CB, 128), jnp.int32),
             pltpu.VMEM((2, NB, CB * 128), BF16),
             pltpu.VMEM((CB, HALF, 256), BF16),
-            pltpu.VMEM((GROUPS, N_ROW, NB // N_ROW, 256), BF16),
-            pltpu.VMEM((GROUPS, N_ROW - 1, NB // N_ROW, 256), BF16),
-            pltpu.VMEM((N_COL * 8, 128), F32),
-            pltpu.VMEM((N_COL - 1, 8, 128), F32),
+            *[pltpu.VMEM((NEAR, FAR, 2 * count), BF16) for _, count in STACKS],
+            *[pltpu.VMEM((NEAR - 1, FAR, 2 * count), BF16) for _, count in STACKS],
+            pltpu.VMEM((FAR * 16, 128), F32),
+            pltpu.VMEM((FAR - 1, 16, 128), F32),
             pltpu.VMEM(e1.shape, F32),
             pltpu.VMEM(e2.shape, BF16),
             dma((5,)), dma((ROUNDS,)), dma((ROUNDS,)),
             dma((3, PIECES)), dma((3, PIECES)), dma((PIECES,)), dma((PIECES,)),
-            dma((GROUPS, N_ROW - 1)), dma((GROUPS, N_ROW - 1)), dma((N_COL - 1,)), dma((N_COL - 1,)),
+            dma((len(STACKS), NEAR - 1)), dma((len(STACKS), NEAR - 1)), dma((FAR - 1,)), dma((FAR - 1,)),
+            pltpu.SemaphoreType.REGULAR,
         ],
         compiler_params=pltpu.CompilerParams(
-            collective_id=0, has_side_effects=True, vmem_limit_bytes=64 << 20),
+            collective_id=0, has_side_effects=True, vmem_limit_bytes=48 << 20),
         name="correlate",
-    )(dead_mask, spectra, pair_bins, jnp.asarray(e1), jnp.asarray(e2))
+    )(*[
+        pltpu.with_memory_space_constraint(x, pltpu.HBM)
+        for x in (dead_mask, spectra, pair_bins, jnp.asarray(e1), jnp.asarray(e2))
+    ])
 
 
 def solution(mesh):

time: 37.3 us -> 34.5 us (0.925)
  Pallas kernels: 35.9 us -> 33.7 us
  local copies, waits for them, and re-layouts: 1.26 us -> 0.58 us
    pallas_call x1, Pallas kernels: 35.9 us -> 33.7 us  [on_device(): pl.pallas_call(kernel, out_shape=jax.ShapeDtypeStruct((1, LAGS), F32), in...]
    unnamed x1, local copies, waits for them, and re-layouts: 1.26 us -> 0.58 us
where the time goes in v3:
time: 34.5 us; the launch traced here: 34.3 us
  Pallas kernels  33.7 us (98%)
  local copies, waits for them, and re-layouts  0.58 us (2%)
    pallas_call x1, Pallas kernels, on_device(): pl.pallas_call(kernel, out_shape=jax.ShapeDtypeStruct((1, LAGS), F32), in...  33.7 us

profile of v3, /device:TPU:1, one launch (start us, length us, event | category | flops | bytes accessed | tf_op | source)
XLA Modules:
  0.0 34.3 jit_solution(4968122249071584715)
XLA Ops:
  0.0 33.7 %correlate.1 = f32[1,896]{1,0:T(1,128)S(1)} custom-call(s32[32]{0:T(128)} %alive_hbm.1, bf16[32,8,1536]{2,1,0:T(8,128)(2,1)} %spec_hbm.1, s32[4,32,32]{2,1,0:T(8,128)} %bins_hbm.1, f32[2,2,8,384]{3,2,1,0:T(8,128)} %constant.4.clone.e1_hbm, bf16[2,2,768,128]{3,2,1,0:T(8,128)(2,1)} %constant.5.clone.e2_hbm), custom_call_target="tpu_custom_call" | custom-call | tf_op jit(solution)/shard_map/correlate/pallas_call | solution.py:352
  33.8 0.6 %copy.7 = f32[1,896]{1,0:T(1,128)} copy(f32[1,896]{1,0:T(1,128)S(1)} %correlate.1) | data formatting | bytes 7168

commit v4 on v3

--- a/solution.py
+++ b/solution.py
@@ -21,8 +21,8 @@
 FC = 16
 HALF = F // 2
 CHUNKS = HALF // FC
-PIECES = 6
-CP = CHUNKS // PIECES
+SPANS = ((0, 4), (4, 4), (8, 4), (12, 4), (16, 4), (20, 2), (22, 2))
+PIECES = len(SPANS)
 LAG = 4
 GROUPS = HALF // 128
 NEAR = 8
@@ -52,11 +52,17 @@
     return e1, np.stack([high, low], axis=0)
 
 
-def flip(value, mask):
-    for bit in range(4):
-        if mask >> bit & 1:
-            value = value + (1 << bit) * (1 - 2 * ((value // (1 << bit)) % 2))
-    return value
+def flipper(value, bits):
+    steps = [(1 << bit) * (1 - 2 * ((value // (1 << bit)) % 2)) for bit in range(bits)]
+
+    def flip(mask):
+        result = value
+        for bit in range(bits):
+            if mask >> bit & 1:
+                result = result + steps[bit]
+        return result
+
+    return flip
 
 
 def links(mask):
@@ -71,7 +77,7 @@
 
 def kernel(
     alive_hbm, spec_hbm, bins_hbm, e1_hbm, e2_hbm, out_ref,
-    alive_ref, bins_ref, scale_v, x_v, d_v, send_v, recv_v, pbs_v, pbr_v, oh_v, cross_v, part0_v, part1_v, near0_v, near1_v, s2_v, r2_v, e1_v, e2_v,
+    alive_ref, bins_ref, scale_v, x_v, d_v, send_v, recv_v, lhs_v, pbs_v, pbr_v, oh_v, cross_v, part0_v, part1_v, near0_v, near1_v, s2_v, r2_v, e1_v, e2_v,
     local_sem, pb_ss, pb_rs, a_ss, a_rs, f_ss, f_rs, near_ss, near_rs, far_ss, far_rs, entered,
 ):
     parts, nears = (part0_v, part1_v), (near0_v, near1_v)
@@ -81,8 +87,11 @@
     far = row * 2 + col // 2 % 2
     parity = (col + col // 2 + col // 4 + col // 8) % 2
 
+    flip_row, flip_col, flip_near, flip_far = (
+        flipper(value, bits) for value, bits in ((row, 3), (col, 4), (near, 3), (far, 4)))
+
     def device(mask):
-        return (flip(row, mask >> 4), flip(col, mask & 15))
+        return (flip_row(mask >> 4), flip_col(mask & 15))
 
     loads = [
         pltpu.make_async_copy(source, target, local_sem.at[n])
@@ -130,7 +139,7 @@
         lax.fori_loop(0, CB, one, 0, unroll=8)
 
     def span(piece):
-        return pl.ds(piece * CP, CP)
+        return pl.ds(*SPANS[piece])
 
     def core_copy(piece):
         return pltpu.make_async_remote_copy(
@@ -171,27 +180,43 @@
 
         lax.fori_loop(0, 8, pack, 0, unroll=2)
 
-        @pl.when(group == 0)
-        def _():
+        if group == 0:
             pl.semaphore_wait(barrier, len(peers))
             for copy in bin_copies:
                 copy.start()
 
-        pieces = [group * (8 // CP) + k for k in range(8 // CP)]
+        pieces = [k for k, (first, _) in enumerate(SPANS) if first // 8 == group]
         for piece in pieces:
             for make in (x_copy, z_copy, core_copy):
                 make(piece).start()
 
-        @pl.when(group == 0)
-        def _():
+        if group == 0:
             for along_z in (2, 16, 18):
                 pl.semaphore_signal(entered, inc=1, device_id=device(along_z), device_id_type=MESH)
         return 0
 
-    lax.fori_loop(0, GROUPS, send, 0)
+    for group in range(GROUPS):
+        send(group, 0)
+
+    mask = (
+        lax.broadcasted_iota(jnp.int32, (FC, 256), 1) % FC == lax.broadcasted_iota(jnp.int32, (FC, 256), 0)
+    ).astype(F32).astype(BF16)
+
+    def spread(q):
+        start = (parity * CHUNKS + q) * CB
+        for i in range(CB):
+            v = [d_v[c, pl.ds(start + i, 8, stride=0), :] for c in range(2)]
+            v = jnp.concatenate([jnp.concatenate([u, u], axis=0).astype(BF16) for u in v], axis=1)
+            lhs_v[q, i * FC : i * FC + FC, :] = v * mask
 
     def rest(group, _):
         whiten(parity * GROUPS + group)
+
+        def one(k, _):
+            spread(group * 8 + k)
+            return 0
+
+        lax.fori_loop(0, 8, one, 0, unroll=2)
         return 0
 
     lax.fori_loop(0, GROUPS, rest, 0)
@@ -220,22 +245,11 @@
     for k in range(2, LAG):
         forward(k)
 
-    mask = (
-        lax.broadcasted_iota(jnp.int32, (FC, 256), 1) % FC == lax.broadcasted_iota(jnp.int32, (FC, 256), 0)
-    ).astype(F32).astype(BF16)
-
     def products(q, _):
-        start = (parity * CHUNKS + q) * CB
-        parts = []
-        for i in range(CB):
-            v = [d_v[c, pl.ds(start + i, 8, stride=0), :] for c in range(2)]
-            v = jnp.concatenate([jnp.concatenate([u, u], axis=0).astype(BF16) for u in v], axis=1)
-            parts.append(v * mask)
-        lhs = jnp.concatenate(parts, axis=0)
         other_part = recv_v[:, q].reshape(ROUNDS * CB, 256)
         turned = jnp.concatenate([-other_part[:, 128:], other_part[:, :128]], axis=1)
         rhs = jnp.concatenate([other_part, turned], axis=0)
-        cross = nt_dot(lhs, rhs).astype(BF16)
+        cross = nt_dot(lhs_v[q], rhs).astype(BF16)
         cross_v[:, pl.ds(pl.multiple_of(q * FC, FC), FC), :] = cross.reshape(CB, FC, 256)
         return 0
 
@@ -246,7 +260,7 @@
 
     def near_copy(g, k):
         return pltpu.make_async_remote_copy(
-            src_ref=parts[g].at[flip(near, k)], dst_ref=nears[g].at[k - 1],
+            src_ref=parts[g].at[flip_near(k)], dst_ref=nears[g].at[k - 1],
             send_sem=near_ss.at[g, k - 1], recv_sem=near_rs.at[g, k - 1],
             device_id=device(near_mask[k]), device_id_type=MESH)
 
@@ -255,36 +269,31 @@
         for c in range(2):
             values = jnp.concatenate(
                 [cross_v[i, first : first + count, c * 128 : c * 128 + 128] for i in range(CB)], axis=1)
-            total = nt_dot(oh_v[c], values)
+            total = nt_dot(values, oh_v[c]).T
             parts[g][:, :, c * count : c * count + count] = total.astype(BF16).reshape(NEAR, FAR, count)
         for k in near_order:
             near_copy(g, k).start()
 
-    def step(piece, _):
-        @pl.when(piece < PIECES)
-        def _():
+    for piece in range(LAG, PIECES + LAG):
+        if piece < PIECES:
             forward(piece)
-
         before = piece - LAG
         core_copy(before).wait_recv()
         z_copy(before).wait_recv()
         x_forward(before).wait_recv()
-        lax.fori_loop(0, CP, lambda k, _: products(before * CP + k, _), 0, unroll=CP)
-
+        begin, number = SPANS[before]
+        lax.fori_loop(0, number, lambda k, _: products(begin + k, _), 0, unroll=number)
         for g, (first, count) in enumerate(STACKS):
-            @pl.when(before == (first + count) // (FC * CP) - 1)
-            def _():
+            if (begin + number) * FC == first + count:
                 stack(g)
-        return 0
-
-    lax.fori_loop(LAG, PIECES + LAG, step, 0)
 
     def drain(piece, _):
         for make in (core_copy, x_copy, z_copy, x_forward):
             make(piece).wait_send()
         return 0
 
-    lax.fori_loop(0, PIECES, drain, 0)
+    for piece in range(PIECES):
+        drain(piece, 0)
 
     for g, (first, count) in enumerate(STACKS):
         totals = [parts[g][near].astype(F32), None]
@@ -303,7 +312,7 @@
 
     far_copies = [
         pltpu.make_async_remote_copy(
-            src_ref=s2_v.at[pl.ds(pl.multiple_of(flip(far, k) * 16, 16), 16), :], dst_ref=r2_v.at[k - 1],
+            src_ref=s2_v.at[pl.ds(pl.multiple_of(flip_far(k) * 16, 16), 16), :], dst_ref=r2_v.at[k - 1],
             send_sem=far_ss.at[k - 1], recv_sem=far_rs.at[k - 1],
             device_id=device(far_mask[k]), device_id_type=MESH)
         for k in far_order
@@ -362,6 +371,7 @@
             pltpu.VMEM((2, 2 * CHUNKS * CB, 128), F32),
             pltpu.VMEM((CHUNKS, CB, 256), BF16),
             pltpu.VMEM((ROUNDS, CHUNKS, CB, 256), BF16),
+            pltpu.VMEM((CHUNKS, CB * FC, 256), BF16),
             pltpu.VMEM((CB, 128), jnp.int32),
             pltpu.VMEM((ROUNDS, CB, 128), jnp.int32),
             pltpu.VMEM((2, NB, CB * 128), BF16),

time: 34.5 us -> 34.2 us (level)
  no operation moved by 1% of the time
where the time goes in v4:
time: 34.2 us; the launch traced here: 34 us
  Pallas kernels  33.4 us (98%)
  local copies, waits for them, and re-layouts  0.58 us (2%)
    pallas_call x1, Pallas kernels, on_device(): pl.pallas_call(kernel, out_shape=jax.ShapeDtypeStruct((1, LAGS), F32), in...  33.4 us

profile of v4, /device:TPU:1, one launch (start us, length us, event | category | flops | bytes accessed | tf_op | source)
XLA Modules:
  0.0 34.0 jit_solution(7958489641689082105)
XLA Ops:
  0.0 33.4 %correlate.1 = f32[1,896]{1,0:T(1,128)S(1)} custom-call(s32[32]{0:T(128)} %alive_hbm.1, bf16[32,8,1536]{2,1,0:T(8,128)(2,1)} %spec_hbm.1, s32[4,32,32]{2,1,0:T(8,128)} %bins_hbm.1, f32[2,2,8,384]{3,2,1,0:T(8,128)} %constant.4.clone.e1_hbm, bf16[2,2,768,128]{3,2,1,0:T(8,128)(2,1)} %constant.5.clone.e2_hbm), custom_call_target="tpu_custom_call" | custom-call | tf_op jit(solution)/shard_map/correlate/pallas_call | solution.py:361
  33.4 0.6 %copy.7 = f32[1,896]{1,0:T(1,128)} copy(f32[1,896]{1,0:T(1,128)S(1)} %correlate.1) | data formatting | bytes 7168

commit v5 on v4

--- a/solution.py
+++ b/solution.py
@@ -368,7 +368,7 @@
             pltpu.VMEM((ROUNDS, CB, CB), jnp.int32),
             pltpu.VMEM((CB, W, 128), F32),
             pltpu.VMEM((CB, W, 2 * F), BF16),
-            pltpu.VMEM((2, 2 * CHUNKS * CB, 128), F32),
+            pltpu.VMEM((2, 2 * CHUNKS * CB + 64, 128), F32),
             pltpu.VMEM((CHUNKS, CB, 256), BF16),
             pltpu.VMEM((ROUNDS, CHUNKS, CB, 256), BF16),
             pltpu.VMEM((CHUNKS, CB * FC, 256), BF16),
@@ -378,7 +378,7 @@
             pltpu.VMEM((CB, HALF, 256), BF16),
             *[pltpu.VMEM((NEAR, FAR, 2 * count), BF16) for _, count in STACKS],
             *[pltpu.VMEM((NEAR - 1, FAR, 2 * count), BF16) for _, count in STACKS],
-            pltpu.VMEM((FAR * 16, 128), F32),
+            pltpu.VMEM((FAR * 16 + 16, 128), F32),
             pltpu.VMEM((FAR - 1, 16, 128), F32),
             pltpu.VMEM(e1.shape, F32),
             pltpu.VMEM(e2.shape, BF16),

time: 34.2 us -> 34.2 us (level)
  no operation moved by 1% of the time
where the time goes in v5:
time: 34.2 us; the launch traced here: 34 us
  Pallas kernels  33.4 us (98%)
  local copies, waits for them, and re-layouts  0.58 us (2%)
    pallas_call x1, Pallas kernels, on_device(): pl.pallas_call(kernel, out_shape=jax.ShapeDtypeStruct((1, LAGS), F32), in...  33.4 us

profile of v5, /device:TPU:1, one launch (start us, length us, event | category | flops | bytes accessed | tf_op | source)
XLA Modules:
  0.0 34.0 jit_solution(16336169011489441587)
XLA Ops:
  0.0 33.4 %correlate.1 = f32[1,896]{1,0:T(1,128)S(1)} custom-call(s32[32]{0:T(128)} %alive_hbm.1, bf16[32,8,1536]{2,1,0:T(8,128)(2,1)} %spec_hbm.1, s32[4,32,32]{2,1,0:T(8,128)} %bins_hbm.1, f32[2,2,8,384]{3,2,1,0:T(8,128)} %constant.4.clone.e1_hbm, bf16[2,2,768,128]{3,2,1,0:T(8,128)(2,1)} %constant.5.clone.e2_hbm), custom_call_target="tpu_custom_call" | custom-call | tf_op jit(solution)/shard_map/correlate/pallas_call | solution.py:361
  33.4 0.6 %copy.7 = f32[1,896]{1,0:T(1,128)} copy(f32[1,896]{1,0:T(1,128)S(1)} %correlate.1) | data formatting | bytes 7168
